TPU v7x, 256 devices: a whole 4x4x8 slice. The times are simulated.
256 devices in a mesh: row: 16 (over z, core), col: 16 (over y, x).
Axes of the slice: x: 4, y: 4, z: 8, core: 2. Of those that a mesh axis runs over, the one named last changes fastest.
Arguments:
- clean_in: bfloat16 [512, 8192], P('row', 'col'), may hold values from -6 to 6
- corrupt_in: bfloat16 [512, 8192], P('row', 'col'), may hold values from -6 to 6
- patch_mask: int32 [512], replicated, may hold values 0 or 1
- gate_weight: bfloat16 [8192, 28672], P('col', 'row'), may hold values from -0.0625 to 0.0625
- up_weight: bfloat16 [8192, 28672], P('col', 'row'), may hold values from -0.0625 to 0.0625
- down_weight: bfloat16 [28672, 8192], P('row', 'col'), may hold values from -0.03125 to 0.03125
Outputs:
- clean_out: float32 [512, 8192], P('row', 'col')
- patched_out: float32 [512, 8192], P('row', 'col')
All inputs are finite; a program needn't handle non-finite values.
Results may differ from a plain program's by a relative error of at most 0.0029.
Values may be sent and summed in bfloat16 or wider, within the bound.
A program may use at most 128 MiB of HBM per device.

v0:
```python
import jax
import jax.numpy as jnp
from jax import lax
from jax.sharding import PartitionSpec as P


def on_device(clean_in, corrupt_in, patch_mask, gate_weight, up_weight, down_weight):
    stacked = jnp.stack((clean_in, corrupt_in), axis=1)
    piece = lax.all_gather(stacked, "row", axis=0, tiled=True)
    gate_part = jnp.einsum("tkd,df->tkf", piece, gate_weight, preferred_element_type=jnp.float32)
    up_part = jnp.einsum("tkd,df->tkf", piece, up_weight, preferred_element_type=jnp.float32)
    partial_sums = jnp.stack((gate_part, up_part), axis=2)
    summed = lax.psum_scatter(partial_sums, "col", scatter_dimension=0, tiled=True)
    row_count = summed.shape[0]
    row_mask = lax.dynamic_slice_in_dim(patch_mask, lax.axis_index("col") * row_count, row_count, 0)
    hidden = (jax.nn.silu(summed[:, :, 0]) * summed[:, :, 1]).astype(jnp.bfloat16)
    patched = jnp.where(row_mask[:, None] == 1, hidden[:, 0], hidden[:, 1])
    paired = jnp.stack((hidden[:, 0], patched), axis=1)
    gathered = lax.all_gather(paired, "col", axis=0, tiled=True)
    result = lax.psum_scatter(
        jnp.einsum("tkf,fd->tkd", gathered, down_weight, preferred_element_type=jnp.float32),
        "row",
        scatter_dimension=0,
        tiled=True,
    )
    return (result[:, 0], result[:, 1])


def solution(mesh):
    placed = (
        P("row", "col"),
        P("row", "col"),
        P(),
        P("col", "row"),
        P("col", "row"),
        P("row", "col"),
    )
    return jax.shard_map(
        on_device,
        mesh=mesh,
        in_specs=placed,
        out_specs=(P("row", "col"), P("row", "col")),
        check_vma=False,
    )
```

profile of v0, /device:TPU:2, one launch (start us, length us, event | category | flops | bytes accessed | tf_op | source)
XLA Modules:
  0.0 311.0 jit_solution(6040133685950640488)
XLA Ops:
  7.2 0.0 copy-start
  7.2 0.0 all-gather.3.cloned.1.call-start
  7.2 1.5 pad_maximum_fusion.2
  8.8 0.0 all-gather.3.cloned.1.call-update
  8.8 0.0 reduce-scatter.3.cloned.1.call-start
  8.8 43.1 %all-gather.3.cloned.1.call-done = bf16[512,2,512]{2,0,1:T(8,128)(2,1)} async-done(((bf16[32,2,512]{2,0,1:T(8,128)(2,1)}), bf16[512,2,512]{2,0,1:T(8,128)(2,1)}) %all-gather.3.cloned.1.call-update) | async-done | bytes 1048592 | tf_op jit(solution)/shard_map/all_gather | solution.py:9
  52.0 0.0 copy-done
  52.0 0.0 copy-start.1
  52.0 0.0 copy-start.2
  52.0 6.4 %convolution_bitcast_fusion = f32[512,2,1,1792]{3,0,1,2:T(8,128)} fusion(bf16[512,2,512]{2,0,1:T(8,128)(2,1)} %all-gather.3.cloned.1.call-done, bf16[512,1792]{1,0:T(8,128)(2,1)S(1)} %copy-done), kind=kOutput, calls=%fused_computation.1 | convolution fusion | flops 1879048192 | bytes 10223616 | tf_op jit(solution)/shard_map/tkd,df->tkf/dot_general | solution.py:11
  58.3 0.0 copy-done.1
  58.3 0.0 copy-done.2
  58.3 5.0 %convolution_bitcast_fusion.1 = f32[512,2,1,1792]{3,0,1,2:T(8,128)} fusion(bf16[512,2,512]{2,0,1:T(8,128)(2,1)S(1)} %copy-done.2, bf16[512,1792]{1,0:T(8,128)(2,1)S(1)} %copy-done.1), kind=kOutput, calls=%fused_computation.2 | convolution fusion | flops 1879048192 | bytes 10223616 | tf_op jit(solution)/shard_map/tkd,df->tkf/dot_general | solution.py:10
  63.4 11.9 %pad_maximum_fusion = f32[512,2,2,1792]{3,0,1,2:T(8,128)} fusion(f32[512,2,1,1792]{3,0,1,2:T(8,128)} %convolution_bitcast_fusion, f32[512,2,1,1792]{3,0,1,2:T(8,128)} %convolution_bitcast_fusion.1), kind=kLoop, calls=%fused_computation | loop fusion | flops 3670016 | bytes 29360128 | tf_op jit(solution)/shard_map/stack | solution.py:12
  75.3 0.0 reduce-scatter.3.cloned.1.call-update
  75.3 0.0 all-gather.5.cloned.1.call-start
  75.3 0.8 dynamic-slice_compare_fusion
  76.1 104.8 %reduce-scatter.3.cloned.1.call-done = f32[32,2,2,1792]{3,0,1,2:T(8,128)} async-done(((f32[512,2,2,1792]{3,0,1,2:T(8,128)}), f32[32,2,2,1792]{3,0,1,2:T(8,128)}) %reduce-scatter.3.cloned.1.call-update) | async-done | bytes 917520 | tf_op jit(solution)/shard_map/reduce_scatter | solution.py:13
  180.9 1.3 fusion.5
  182.2 0.1 fusion.6
  182.3 0.7 pad_maximum_fusion.1
  183.0 0.0 all-gather.5.cloned.1.call-update
  183.0 0.0 reduce-scatter.5.cloned.1.call-start
  183.1 54.0 %all-gather.5.cloned.1.call-done = bf16[512,2,1792]{2,0,1:T(8,128)(2,1)} async-done(((bf16[32,2,1792]{2,0,1:T(8,128)(2,1)}), bf16[512,2,1792]{2,0,1:T(8,128)(2,1)}) %all-gather.5.cloned.1.call-update) | async-done | bytes 3670032 | tf_op jit(solution)/shard_map/all_gather | solution.py:19
  237.0 6.0 %fusion = f32[512,2,512]{2,0,1:T(8,128)} fusion(bf16[512,2,1792]{2,0,1:T(8,128)(2,1)} %all-gather.5.cloned.1.call-done, bf16[1792,512]{1,0:T(8,128)(2,1)} %param.11), kind=kOutput, calls=%fused_computation.3 | convolution fusion | flops 1879048192 | bytes 7602176 | tf_op jit(solution)/shard_map/tkf,fd->tkd/dot_general | solution.py:21
  243.0 0.0 reduce-scatter.5.cloned.1.call-update
  243.1 59.8 %reduce-scatter.5.cloned.1.call-done = f32[32,2,512]{2,0,1:T(8,128)} async-done(((f32[512,2,512]{2,0,1:T(8,128)}), f32[32,2,512]{2,0,1:T(8,128)}) %reduce-scatter.5.cloned.1.call-update) | async-done | bytes 131088 | tf_op jit(solution)/shard_map/reduce_scatter | solution.py:20
  302.9 1.5 slice_bitcast_fusion.2
Async XLA Ops:
  7.2 44.8 %copy-start = (bf16[512,1792]{1,0:T(8,128)(2,1)S(1)}, bf16[512,1792]{1,0:T(8,128)(2,1)}, u32[]{:S(2)}) copy-start(bf16[512,1792]{1,0:T(8,128)(2,1)} %param.10) | copy-start | bytes 5505028
  7.2 44.8 %all-gather.3.cloned.1.call-start = ((), (), s32[]{:S(2)}) async-start(), calls=%async_computation.2 | async-start | bytes 1114112 | tf_op jit(solution)/shard_map/all_gather | solution.py:9
  8.8 172.1 %reduce-scatter.3.cloned.1.call-start = ((), (), s32[]{:S(2)}) async-start(), calls=%async_computation.3 | async-start | bytes 15597568 | tf_op jit(solution)/shard_map/reduce_scatter | solution.py:13
  52.0 6.4 %copy-start.1 = (bf16[512,1792]{1,0:T(8,128)(2,1)S(1)}, bf16[512,1792]{1,0:T(8,128)(2,1)}, u32[]{:S(2)}) copy-start(bf16[512,1792]{1,0:T(8,128)(2,1)} %param.9) | copy-start | bytes 5505028
  52.0 6.4 %copy-start.2 = (bf16[512,2,512]{2,0,1:T(8,128)(2,1)S(1)}, bf16[512,2,512]{2,0,1:T(8,128)(2,1)}, u32[]{:S(2)}) copy-start(bf16[512,2,512]{2,0,1:T(8,128)(2,1)} %all-gather.3.cloned.1.call-done) | copy-start | bytes 3145732
  75.3 161.8 %all-gather.5.cloned.1.call-start = ((), (), s32[]{:S(2)}) async-start(), calls=%async_computation.4 | async-start | bytes 3899392 | tf_op jit(solution)/shard_map/all_gather | solution.py:19
  183.0 119.9 %reduce-scatter.5.cloned.1.call-start = ((), (), s32[]{:S(2)}) async-start(), calls=%async_computation.5 | async-start | bytes 2228224 | tf_op jit(solution)/shard_map/reduce_scatter | solution.py:20
Sparse Core Ops, SparseCore 0:
  10.4 41.5 all-gather.2
  75.4 105.4 reduce-scatter.2
  183.3 53.6 all-gather.4
  243.2 59.6 reduce-scatter.4
where the time goes:
time: 311 us
  waiting for transfers between devices  262 us (84%)
  matrix products  17.4 us (6%)
  other arithmetic  16.3 us (5%)
  between operations  13.8 us (4%)
    reduce_scatter x1, waiting for transfers between devices, on_device(): lax.psum_scatter(partial_sums, 'col', scatter_dimension=0, tiled=True)  105 us
    reduce_scatter x1, waiting for transfers between devices, on_device(): lax.psum_scatter(jnp.einsum('tkf,fd->tkd', gathered, down_weight, preferr...  59.8 us
    all_gather x1, waiting for transfers between devices, on_device(): gathered = lax.all_gather(paired, 'col', axis=0, tiled=True)  54 us
    all_gather x1, waiting for transfers between devices, on_device(): piece = lax.all_gather(stacked, 'row', axis=0, tiled=True)  43.1 us
    another operation x1, other arithmetic, on_device(): partial_sums = jnp.stack((gate_part, up_part), axis=2)  11.9 us
    dot_general x1, matrix products, on_device(): jnp.einsum('tkd,df->tkf', piece, up_weight, preferred_element_type=jnp.fl...  6.36 us
  transfers between devices with their start and end apart: 4, of which 4 were waited for; matrix products, arithmetic and copies ran while one was open for 0% of the time, Pallas kernels for 0%

commit v1 on v0

--- a/solution.py
+++ b/solution.py
@@ -6,7 +6,14 @@
 
 def on_device(clean_in, corrupt_in, patch_mask, gate_weight, up_weight, down_weight):
     stacked = jnp.stack((clean_in, corrupt_in), axis=1)
-    piece = lax.all_gather(stacked, "row", axis=0, tiled=True)
+
+    def feed_files(s0):
+        w2 = jnp.stack([s0 for _ in range(lax.axis_size("row"))])
+        plain = lax.all_to_all(w2, axis_name="row", split_axis=0, concat_axis=0)
+        work_now = jnp.concatenate(plain, 0)
+        return work_now
+
+    piece = feed_files(stacked)
     gate_part = jnp.einsum("tkd,df->tkf", piece, gate_weight, preferred_element_type=jnp.float32)
     up_part = jnp.einsum("tkd,df->tkf", piece, up_weight, preferred_element_type=jnp.float32)
     partial_sums = jnp.stack((gate_part, up_part), axis=2)

time: 311 us -> 302 us (0.971)
  waiting for transfers between devices: 262 us -> 219 us
  blocking collectives: 0 us -> 35.5 us
    all_gather x1 -> x0, waiting for transfers between devices: 43.1 us -> none  [on_device(): piece = lax.all_gather(stacked, 'row', axis=0, tiled=True)]
    all_to_all x0 -> x1, blocking collectives: none -> 35.5 us  [feed_files(): plain = lax.all_to_all(w2, axis_name='row', split_axis=0, concat_axis=0)]
  transfers between devices with their start and end apart: 4 -> 3, of which waited for: 4 -> 3; matrix products, arithmetic and copies ran while one was open for 0% -> 0% of each run, Pallas kernels for 0% -> 0%
where the time goes in v1:
time: 302 us; the launch traced here: 301 us
  waiting for transfers between devices  219 us (73%)
  blocking collectives  35.5 us (12%)
  matrix products  16 us (5%)
  other arithmetic  15.6 us (5%)
  between operations  13.8 us (5%)
    reduce_scatter x1, waiting for transfers between devices, on_device(): lax.psum_scatter(partial_sums, 'col', scatter_dimension=0, tiled=True)  105 us
    reduce_scatter x1, waiting for transfers between devices, on_device(): lax.psum_scatter(jnp.einsum('tkf,fd->tkd', gathered, down_weight, preferr...  59.8 us
    all_gather x1, waiting for transfers between devices, on_device(): gathered = lax.all_gather(paired, 'col', axis=0, tiled=True)  54.1 us
    all_to_all x1, blocking collectives, feed_files(): plain = lax.all_to_all(w2, axis_name='row', split_axis=0, concat_axis=0)  35.5 us
    another operation x1, other arithmetic, on_device(): partial_sums = jnp.stack((gate_part, up_part), axis=2)  11.9 us
  transfers between devices with their start and end apart: 3, of which 3 were waited for; matrix products, arithmetic and copies ran while one was open for 0% of the time, Pallas kernels for 0%

profile of v1, /device:TPU:2, one launch (start us, length us, event | category | flops | bytes accessed | tf_op | source)
XLA Modules:
  0.0 301.4 jit_solution(8329041511735244777)
XLA Ops:
  7.2 0.0 copy-start
  7.2 0.0 reduce-scatter.3.cloned.1.call-start
  7.2 0.9 pad_maximum_fusion.2
  8.1 0.1 stack.19
  8.2 35.5 %all_to_all.5 = bf16[16,32,2,512]{3,1,2,0:T(8,128)(2,1)S(1)} all-to-all(bf16[16,32,2,512]{3,1,2,0:T(8,128)(2,1)S(1)} %stack.19), channel_id=1, replica_groups=mesh['row'=16,'col'=16] {'row'}, dimensions={0} | all-to-all | bytes 2097152 | tf_op jit(solution)/shard_map/all_to_all | solution.py:12
  43.8 0.1 copy.8
  43.9 0.0 copy-done
  43.9 0.0 copy-start.1
  43.9 5.0 %convolution_bitcast_fusion = f32[512,2,1,1792]{3,0,1,2:T(8,128)} fusion(bf16[512,2,512]{2,0,1:T(8,128)(2,1)S(1)} %bitcast.33, bf16[512,1792]{1,0:T(8,128)(2,1)S(1)} %copy-done), kind=kOutput, calls=%fused_computation.1 | convolution fusion | flops 1879048192 | bytes 10223616 | tf_op jit(solution)/shard_map/tkd,df->tkf/dot_general | solution.py:18
  48.9 0.0 copy-done.1
  48.9 5.0 %convolution_bitcast_fusion.1 = f32[512,2,1,1792]{3,0,1,2:T(8,128)} fusion(bf16[512,2,512]{2,0,1:T(8,128)(2,1)S(1)} %bitcast.34, bf16[512,1792]{1,0:T(8,128)(2,1)S(1)} %copy-done.1), kind=kOutput, calls=%fused_computation.2 | convolution fusion | flops 1879048192 | bytes 10223616 | tf_op jit(solution)/shard_map/tkd,df->tkf/dot_general | solution.py:17
  53.9 11.9 %pad_maximum_fusion = f32[512,2,2,1792]{3,0,1,2:T(8,128)} fusion(f32[512,2,1,1792]{3,0,1,2:T(8,128)} %convolution_bitcast_fusion, f32[512,2,1,1792]{3,0,1,2:T(8,128)} %convolution_bitcast_fusion.1), kind=kLoop, calls=%fused_computation | loop fusion | flops 3670016 | bytes 29360128 | tf_op jit(solution)/shard_map/stack | solution.py:19
  65.8 0.0 reduce-scatter.3.cloned.1.call-update
  65.9 0.0 all-gather.2.cloned.1.call-start
  65.9 0.8 dynamic-slice_compare_fusion
  66.7 104.6 %reduce-scatter.3.cloned.1.call-done = f32[32,2,2,1792]{3,0,1,2:T(8,128)} async-done(((f32[512,2,2,1792]{3,0,1,2:T(8,128)}), f32[32,2,2,1792]{3,0,1,2:T(8,128)}) %reduce-scatter.3.cloned.1.call-update) | async-done | bytes 917520 | tf_op jit(solution)/shard_map/reduce_scatter | solution.py:20
  171.3 1.3 fusion.5
  172.6 0.1 fusion.6
  172.7 0.7 pad_maximum_fusion.1
  173.4 0.0 all-gather.2.cloned.1.call-update
  173.4 0.0 reduce-scatter.5.cloned.1.call-start
  173.5 54.1 %all-gather.2.cloned.1.call-done = bf16[512,2,1792]{2,0,1:T(8,128)(2,1)} async-done(((bf16[32,2,1792]{2,0,1:T(8,128)(2,1)}), bf16[512,2,1792]{2,0,1:T(8,128)(2,1)}) %all-gather.2.cloned.1.call-update) | async-done | bytes 3670032 | tf_op jit(solution)/shard_map/all_gather | solution.py:26
  227.5 6.0 %fusion = f32[512,2,512]{2,0,1:T(8,128)} fusion(bf16[512,2,1792]{2,0,1:T(8,128)(2,1)} %all-gather.2.cloned.1.call-done, bf16[1792,512]{1,0:T(8,128)(2,1)} %param.11), kind=kOutput, calls=%fused_computation.3 | convolution fusion | flops 1879048192 | bytes 7602176 | tf_op jit(solution)/shard_map/tkf,fd->tkd/dot_general | solution.py:28
  233.5 0.0 reduce-scatter.5.cloned.1.call-update
  233.5 59.8 %reduce-scatter.5.cloned.1.call-done = f32[32,2,512]{2,0,1:T(8,128)} async-done(((f32[512,2,512]{2,0,1:T(8,128)}), f32[32,2,512]{2,0,1:T(8,128)}) %reduce-scatter.5.cloned.1.call-update) | async-done | bytes 131088 | tf_op jit(solution)/shard_map/reduce_scatter | solution.py:27
  293.4 1.5 slice_bitcast_fusion.2
Async XLA Ops:
  7.2 36.7 %copy-start = (bf16[512,1792]{1,0:T(8,128)(2,1)S(1)}, bf16[512,1792]{1,0:T(8,128)(2,1)}, u32[]{:S(2)}) copy-start(bf16[512,1792]{1,0:T(8,128)(2,1)} %param.10) | copy-start | bytes 5505028
  7.2 164.1 %reduce-scatter.3.cloned.1.call-start = ((), (), s32[]{:S(2)}) async-start(), calls=%async_computation.3 | async-start | bytes 15597568 | tf_op jit(solution)/shard_map/reduce_scatter | solution.py:20
  43.9 5.0 %copy-start.1 = (bf16[512,1792]{1,0:T(8,128)(2,1)S(1)}, bf16[512,1792]{1,0:T(8,128)(2,1)}, u32[]{:S(2)}) copy-start(bf16[512,1792]{1,0:T(8,128)(2,1)} %param.9) | copy-start | bytes 5505028
  65.9 161.7 %all-gather.2.cloned.1.call-start = ((), (), s32[]{:S(2)}) async-start(), calls=%async_computation.4 | async-start | bytes 3899392 | tf_op jit(solution)/shard_map/all_gather | solution.py:26
  173.4 120.0 %reduce-scatter.5.cloned.1.call-start = ((), (), s32[]{:S(2)}) async-start(), calls=%async_computation.5 | async-start | bytes 2228224 | tf_op jit(solution)/shard_map/reduce_scatter | solution.py:27
Sparse Core Ops, SparseCore 0:
  66.0 105.2 reduce-scatter.2
  173.8 53.7 all-gather.1
  233.7 59.6 reduce-scatter.4
